TPU v7x, 32 devices: a whole 2x2x4 slice. The times are simulated.
32 devices in a mesh: node: 8 (over z, core), local: 4 (over y, x).
Axes of the slice: x: 2, y: 2, z: 4, core: 2. Of those that a mesh axis runs over, the one named last changes fastest.
Arguments:
- tokens: bfloat16 [64, 7168], P(('node', 'local')), may hold values from -6 to 6
- expert_ids: int32 [64, 8], P(('node', 'local')), may hold values from 0 to 31, all different within a row; in each aligned block of 8 rows (0 to 7, 8 to 15, ...) at most 4 rows name the same one
- gate_weights: bfloat16 [64, 8], P(('node', 'local')), may hold values from 0.049804688 to 1
- expert_seeds: int32 [32], P('node'), may hold values from 0 to 16777215
Outputs:
- moe_out: bfloat16 [64, 7168], P(('node', 'local'))
Inputs may be any that keep to these rules, and one draw needn't show every extreme that they name: `expert_ids`: each row names 8 different experts. Within the tokens of one node group (aligned blocks of 8 rows), no expert is named by more than 4 rows, a bound that some block reaches.
All inputs are finite; a program needn't handle non-finite values.
Results may differ from a plain program's by a relative error of at most 0.0078.
Values may be sent and summed in bfloat16 or wider, within the bound.
No kernel may reach another device: no remote copies, remote signals or barrier semaphores. Data moves between devices by JAX's collectives and lax.ppermute only.
A program may use at most 128 MiB of HBM per device.

v0:
```python
import math
import jax
import jax.numpy as jnp
from jax import lax
from jax.sharding import PartitionSpec as P

FF = 2048
TOP = 8
EXP_NODE = 4
mix_const = 73244475


def hashed_weights(expert_seed, matrix_code, row_ids, col_ids, col_count, fan_in):
    flat_index = row_ids[:, None] * col_count + col_ids[None, :]
    mixing = expert_seed + matrix_code * 1000003 + flat_index * 374761393
    mixing = mixing ^ jnp.right_shift(mixing, 16)
    mixing = mixing * mix_const
    mixing = mixing ^ jnp.right_shift(mixing, 15)
    mixing = mixing * mix_const
    mixing = mixing ^ jnp.right_shift(mixing, 16)
    uniform_part = (mixing & 16777215).astype(jnp.float32) * (1.0 / 16777216.0) - 0.5
    return (uniform_part * math.sqrt(12.0 / fan_in)).astype(jnp.bfloat16)


def block_weights(expert_seed, hidden_ids, model_width, hidden_total):
    feature_ids = jnp.arange(model_width, dtype=jnp.int32)
    gate_and_up = jnp.concatenate(
        [
            hashed_weights(expert_seed, 0, feature_ids, hidden_ids, hidden_total, model_width),
            hashed_weights(expert_seed, 1, feature_ids, hidden_ids, hidden_total, model_width),
        ],
        axis=1,
    )
    w_down = hashed_weights(expert_seed, 2, hidden_ids, feature_ids, model_width, hidden_total)
    return (gate_and_up, w_down)


def apply_block(row_block, gate_and_up, w_down):
    hidden_block = w_down.shape[0]
    projected = jnp.dot(row_block, gate_and_up, preferred_element_type=jnp.float32)
    hidden = (jax.nn.silu(projected[:, :hidden_block]) * projected[:, hidden_block:]).astype(
        jnp.bfloat16
    )
    return jnp.dot(hidden, w_down, preferred_element_type=jnp.float32)


def quarter_output(flat_rows, expert_seed, first_unit, quarter_width, hidden_block):
    model_width = flat_rows.shape[1]
    accumulated = jnp.zeros((flat_rows.shape[0], model_width), jnp.float32)
    for offset in range(0, quarter_width, hidden_block):
        hidden_ids = first_unit + offset + jnp.arange(hidden_block, dtype=jnp.int32)
        gate_and_up, w_down = block_weights(expert_seed, hidden_ids, model_width, FF)
        accumulated = accumulated + apply_block(flat_rows, gate_and_up, w_down)
    return accumulated.astype(jnp.bfloat16)


def body(tokens, expert_ids, gate_weights, expert_seeds):
    n_node = lax.axis_size("node")
    n_local = lax.axis_size("local")
    quarters = n_local // EXP_NODE
    quarter_width = FF // quarters
    hidden_block = min(quarter_width, 256)
    model_width = tokens.shape[1]
    group_rows, group_ids, group_gates = (
        lax.all_gather(tokens, "local", axis=0, tiled=True),
        lax.all_gather(expert_ids, "local", axis=0, tiled=True),
        lax.all_gather(gate_weights, "local", axis=0, tiled=True),
    )
    tok_node = group_rows.shape[0]
    capacity = 2 * tok_node * TOP // (EXP_NODE * n_node)
    local_index = lax.axis_index("local")
    expert_kind = local_index // quarters
    quarter = local_index % quarters
    targets = (
        jnp.arange(n_node, dtype=jnp.int32)[:, None] * EXP_NODE
        + jnp.arange(EXP_NODE, dtype=jnp.int32)[None, :]
    )
    id_match = group_ids[:, :, None, None] == targets[None, None, :, :]
    routed_hits = jnp.any(id_match, axis=1)
    picked = jnp.sum(
        jnp.where(id_match, group_gates.astype(jnp.float32)[:, :, None, None], 0.0), axis=1
    )
    counts = jnp.cumsum(routed_hits.astype(jnp.int32), axis=0) - 1
    slot_place = jnp.where(routed_hits, counts, -1)
    slot_select = (
        jnp.transpose(slot_place, (1, 2, 0))[:, :, None, :]
        == jnp.arange(capacity, dtype=jnp.int32)[None, None, :, None]
    )
    expert_seed = expert_seeds[expert_kind]
    first_unit = quarter * quarter_width
    own_select = lax.dynamic_index_in_dim(slot_select, expert_kind, 1, keepdims=False)
    own_picked = lax.dynamic_index_in_dim(picked, expert_kind, 2, keepdims=False)
    outgoing = jnp.einsum(
        "mct,td->mcd",
        own_select.astype(jnp.bfloat16),
        group_rows,
        preferred_element_type=jnp.float32,
    ).astype(jnp.bfloat16)
    arrived = lax.all_to_all(outgoing, "node", split_axis=0, concat_axis=0, tiled=True)
    row_total = arrived.shape[0] * arrived.shape[1]
    flat_rows = arrived.reshape(row_total, model_width)
    flat_out = quarter_output(flat_rows, expert_seed, first_unit, quarter_width, hidden_block)
    returned = lax.all_to_all(
        flat_out.reshape(arrived.shape), "node", split_axis=0, concat_axis=0, tiled=True
    )
    combine_weights = own_select.astype(jnp.float32) * own_picked.T[:, None, :]
    partial_term = jnp.einsum(
        "mct,mcd->td",
        combine_weights,
        returned.astype(jnp.float32),
        precision=lax.Precision.HIGHEST,
    )
    own_rows = lax.psum_scatter(partial_term, "local", scatter_dimension=0, tiled=True)
    return own_rows.astype(jnp.bfloat16)


def solution(mesh):
    return jax.shard_map(
        body,
        mesh=mesh,
        in_specs=(
            P(("node", "local"), None),
            P(("node", "local"), None),
            P(("node", "local"), None),
            P("node"),
        ),
        out_specs=P(("node", "local"), None),
        check_vma=False,
    )
```

profile of v0, /device:TPU:0, one launch (start us, length us, event | category | flops | bytes accessed | tf_op | source)
XLA Modules:
  0.0 199.2 jit_solution(6134852472920081447)
XLA Ops:
  0.0 10.1 %all-gather.2 = bf16[4,2,7168]{2,1,0:T(2,128)(2,1)S(1)} all-gather(bf16[1,2,7168]{2,1,0:T(2,128)(2,1)} %bitcast.32), channel_id=1, replica_groups=mesh['node'=8,'local'=4] {'local'}, dimensions={0}, use_global_device_ids=true | all-gather | bytes 143360 | tf_op jit(solution)/shard_map/all_gather | solution.py:65
  10.2 7.9 %all-gather = s32[4,2,8]{2,1,0:T(2,128)S(1)} all-gather(s32[1,2,8]{2,1,0:T(2,128)} %bitcast.35), channel_id=1, replica_groups=mesh['node'=8,'local'=4] {'local'}, dimensions={0}, use_global_device_ids=true | all-gather | bytes 320 | tf_op jit(solution)/shard_map/all_gather | solution.py:66
  18.1 0.1 compare_reduce_fusion
  18.2 0.1 copy.16
  18.3 0.3 convolution_convert_fusion
  18.6 1.1 copy.18
  19.7 4.9 %all-to-all-start = ((bf16[8,4,7168]{2,1,0:T(4,128)(2,1)}), bf16[8,4,7168]{2,1,0:T(4,128)(2,1)S(1)}, u32[]{:S(2)}, u32[]{:S(2)}) async-start(bf16[8,4,7168]{2,1,0:T(4,128)(2,1)} %copy.18), calls=%async_computation | async-start | bytes 917504 | tf_op jit(solution)/shard_map/all_to_all | solution.py:99
  24.6 1.2 dynamic_slice.13
  26.5 69.3 %fusion.176 = (bf16[7168,256]{1,0:T(8,128)(2,1)}, bf16[7168,256]{1,0:T(8,128)(2,1)}, bf16[7168,256]{1,0:T(8,128)(2,1)}, bf16[7168,256]{1,0:T(8,128)(2,1)}, bf16[...) fusion(s32[256]{0:T(256)S(1)} %get-tuple-element.33, ...), kind=kLoop, calls=%fused_computation.257 | loop fusion | flops 469762048 | bytes 58756104 | tf_op jit(solution)/shard_map/convert_element_type | solution.py:22
  96.6 0.0 all-to-all-done
  96.6 0.1 reshape.115
  96.7 0.0 copy-start.12
  96.7 0.0 copy-start.13
  96.8 4.5 %fusion.193 = f32[32,512]{1,0:T(8,128)S(1)} fusion(bf16[32,7168]{1,0:T(8,128)(2,1)S(1)} %reshape.115, bf16[7168,256]{1,0:T(8,128)(2,1)} %get-tuple-element.31, bf16[7168,256]{1,0:T(8,128)(2,1)} %get-tuple-element.32), kind=kOutput, calls=%fused_computation.274 | convolution fusion | flops 249561088 | bytes 7864320 | tf_op jit(solution)/shard_map/dot_general | solution.py:40
  101.3 0.0 copy-done.12
  101.3 0.7 copy-done.13
  102.1 0.0 copy-start.10
  102.1 0.0 copy-start.11
  102.1 1.3 fusion.197
  103.4 0.7 copy-done.10
  104.1 1.1 copy-done.11
  105.2 0.0 copy-start.8
  105.2 0.0 copy-start.9
  105.2 1.3 fusion.201
  106.6 0.7 copy-done.8
  107.3 1.1 copy-done.9
  108.4 0.0 copy-start.6
  108.4 0.0 copy-start.7
  108.4 1.3 fusion.205
  109.7 0.7 copy-done.6
  110.4 1.1 copy-done.7
  111.5 0.0 copy-start.4
  111.5 0.0 copy-start.5
  111.5 1.3 fusion.209
  112.9 0.7 copy-done.4
  113.6 1.1 copy-done.5
  114.7 1.3 fusion.213
  116.0 0.7 copy-done.2
  116.7 1.1 copy-done.3
  117.9 1.3 fusion.217
  119.2 0.7 copy-done
  119.9 1.1 copy-done.1
  121.0 1.3 fusion.221
  122.4 4.4 %fusion.302 = f32[32,7168]{1,0:T(8,128)S(1)} fusion(s32[256]{0:T(256)S(1)} %iota_multiply_fusion.1, s32[]{:T(128)S(6)} %add.686, f32[32,512]{1,0:T(8,128)S(1)} %fusion.193), kind=kOutput, calls=%fused_computation.384 | convolution fusion | flops 148684800 | bytes 984068 | tf_op jit(solution)/shard_map/dot_general | solution.py:44
  126.8 4.6 %convolution_add_fusion.6 = f32[32,7168]{1,0:T(8,128)S(1)} fusion(f32[32,7168]{1,0:T(8,128)S(1)} %fusion.302, s32[256]{0:T(256)S(1)} %broadcast_multiply_fusion.6, s32[]{:T(128)S(6)} %add.686, f32[32,512]{1,0:T(8,128)S(1)} %fusion.197), kind=kOutput, calls=%fused_computation.78 | convolution fusion | flops 148914176 | bytes 1901572 | tf_op jit(solution)/shard_map/dot_general | solution.py:44
  131.4 4.4 %convolution_add_fusion.5 = f32[32,7168]{1,0:T(8,128)S(1)} fusion(f32[32,7168]{1,0:T(8,128)S(1)} %convolution_add_fusion.6, s32[256]{0:T(256)S(1)} %broadcast_multiply_fusion.5, s32[]{:T(128)S(6)} %add.686, f32[32,512]{1,0:T(8,128)S(1)} %fusion.201), kind=kOutput, calls=%fused_computation.77 | convolution fusion | flops 148914176 | bytes 1901572 | tf_op jit(solution)/shard_map/dot_general | solution.py:44
  135.8 4.4 %convolution_add_fusion.4 = f32[32,7168]{1,0:T(8,128)S(1)} fusion(f32[32,7168]{1,0:T(8,128)S(1)} %convolution_add_fusion.5, s32[256]{0:T(256)S(1)} %broadcast_multiply_fusion.4, s32[]{:T(128)S(6)} %add.686, f32[32,512]{1,0:T(8,128)S(1)} %fusion.205), kind=kOutput, calls=%fused_computation.76 | convolution fusion | flops 148914176 | bytes 1901572 | tf_op jit(solution)/shard_map/dot_general | solution.py:44
  140.3 4.7 %convolution_add_fusion.3 = f32[32,7168]{1,0:T(8,128)S(1)} fusion(f32[32,7168]{1,0:T(8,128)S(1)} %convolution_add_fusion.4, s32[256]{0:T(256)S(1)} %broadcast_multiply_fusion.3, s32[]{:T(128)S(6)} %add.686, f32[32,512]{1,0:T(8,128)S(1)} %fusion.209), kind=kOutput, calls=%fused_computation.75 | convolution fusion | flops 148914176 | bytes 1901572 | tf_op jit(solution)/shard_map/dot_general | solution.py:44
  144.9 4.4 %convolution_add_fusion.2 = f32[32,7168]{1,0:T(8,128)S(1)} fusion(f32[32,7168]{1,0:T(8,128)S(1)} %convolution_add_fusion.3, s32[256]{0:T(256)S(1)} %broadcast_multiply_fusion.2, s32[]{:T(128)S(6)} %add.686, f32[32,512]{1,0:T(8,128)S(1)} %fusion.213), kind=kOutput, calls=%fused_computation.74 | convolution fusion | flops 148914176 | bytes 1901572 | tf_op jit(solution)/shard_map/dot_general | solution.py:44
  149.4 4.7 %convolution_add_fusion.1 = f32[32,7168]{1,0:T(8,128)S(1)} fusion(f32[32,7168]{1,0:T(8,128)S(1)} %convolution_add_fusion.2, s32[256]{0:T(256)S(1)} %broadcast_multiply_fusion.1, s32[]{:T(128)S(6)} %add.686, f32[32,512]{1,0:T(8,128)S(1)} %fusion.217), kind=kOutput, calls=%fused_computation.73 | convolution fusion | flops 148914176 | bytes 1901572 | tf_op jit(solution)/shard_map/dot_general | solution.py:44
  154.1 0.0 copy-start.15
  154.1 4.5 %fusion = bf16[32,7168]{1,0:T(8,128)(2,1)S(1)} fusion(f32[32,7168]{1,0:T(8,128)S(1)} %convolution_add_fusion.1, s32[256]{0:T(256)S(1)} %broadcast_multiply_fusion, s32[]{:T(128)S(6)} %add.686, f32[32,512]{1,0:T(8,128)S(1)} %fusion.221), kind=kOutput, calls=%fused_computation.79 | convolution fusion | flops 149143552 | bytes 1442820 | tf_op jit(solution)/shard_map/dot_general | solution.py:44
  158.6 1.0 reshape.116
  159.5 5.1 %all-to-all-start.1 = ((bf16[8,4,7168]{2,1,0:T(4,128)(2,1)}), bf16[8,4,7168]{2,1,0:T(4,128)(2,1)S(1)}, u32[]{:S(2)}, u32[]{:S(2)}) async-start(bf16[8,4,7168]{2,1,0:T(4,128)(2,1)} %reshape.116), calls=%async_computation.1 | async-start | bytes 917504 | tf_op jit(solution)/shard_map/all_to_all | solution.py:103
  164.6 0.0 copy-done.14
  164.6 7.2 %all-gather.1 = bf16[4,2,8]{2,1,0:T(2,128)(2,1)S(1)} all-gather(bf16[1,2,8]{2,1,0:T(2,128)(2,1)S(1)} %bitcast.36), channel_id=1, replica_groups=mesh['node'=8,'local'=4] {'local'}, dimensions={0}, use_global_device_ids=true | all-gather | bytes 160 | tf_op jit(solution)/shard_map/all_gather | solution.py:67
  171.8 0.1 fusion.307
  172.0 0.1 copy.17
  172.0 0.0 copy-done.15
  172.0 0.6 dynamic-slice
  173.3 5.3 %all-to-all-done.1 = bf16[8,4,7168]{2,1,0:T(4,128)(2,1)S(1)} async-done(((bf16[8,4,7168]{2,1,0:T(4,128)(2,1)}), bf16[8,4,7168]{2,1,0:T(4,128)(2,1)S(1)}, u32[]{:S(2)}, u32[]{:S(2)}) %all-to-all-start.1) | async-done | bytes 458784 | tf_op jit(solution)/shard_map/all_to_all | solution.py:103
  178.6 0.4 convolution_bitcast_fusion
  178.9 19.3 %all-reduce.2 = bf16[8,7168]{1,0:T(8,128)(2,1)S(1)} all-reduce(f32[8,7168]{1,0:T(8,128)S(1)} %convolution_bitcast_fusion), channel_id=2, replica_groups=mesh['node'=8,'local'=4] {'local'}, use_global_device_ids=true, to_apply=%region_3.4.clone | all-reduce | flops 57344 | bytes 344064
  198.2 0.6 dynamic-slice_convert_fusion
  (25 shorter events, 0.1 us)
Async XLA Ops:
  19.7 76.9 %all-to-all-start = ((bf16[8,4,7168]{2,1,0:T(4,128)(2,1)}), bf16[8,4,7168]{2,1,0:T(4,128)(2,1)S(1)}, u32[]{:S(2)}, u32[]{:S(2)}) async-start(bf16[8,4,7168]{2,1,0:T(4,128)(2,1)} %copy.18), calls=%async_computation | async-start | bytes 917504 | tf_op jit(solution)/shard_map/all_to_all | solution.py:99
  96.7 4.6 %copy-start.12 = (bf16[7168,256]{1,0:T(8,128)(2,1)S(1)}, bf16[7168,256]{1,0:T(8,128)(2,1)}, u32[]{:S(2)}) copy-start(bf16[7168,256]{1,0:T(8,128)(2,1)} %get-tuple-element.19) | copy-start | bytes 11010052
  96.7 5.3 %copy-start.13 = (bf16[7168,256]{1,0:T(8,128)(2,1)S(1)}, bf16[7168,256]{1,0:T(8,128)(2,1)}, u32[]{:S(2)}) copy-start(bf16[7168,256]{1,0:T(8,128)(2,1)} %get-tuple-element.20) | copy-start | bytes 11010052
  102.1 2.0 %copy-start.10 = (bf16[7168,256]{1,0:T(8,128)(2,1)S(1)}, bf16[7168,256]{1,0:T(8,128)(2,1)}, u32[]{:S(2)}) copy-start(bf16[7168,256]{1,0:T(8,128)(2,1)} %get-tuple-element.21) | copy-start | bytes 11010052
  102.1 3.2 %copy-start.11 = (bf16[7168,256]{1,0:T(8,128)(2,1)S(1)}, bf16[7168,256]{1,0:T(8,128)(2,1)}, u32[]{:S(2)}) copy-start(bf16[7168,256]{1,0:T(8,128)(2,1)} %get-tuple-element.22) | copy-start | bytes 11010052
  105.2 2.0 %copy-start.8 = (bf16[7168,256]{1,0:T(8,128)(2,1)S(1)}, bf16[7168,256]{1,0:T(8,128)(2,1)}, u32[]{:S(2)}) copy-start(bf16[7168,256]{1,0:T(8,128)(2,1)} %get-tuple-element.23) | copy-start | bytes 11010052
  105.2 3.2 %copy-start.9 = (bf16[7168,256]{1,0:T(8,128)(2,1)S(1)}, bf16[7168,256]{1,0:T(8,128)(2,1)}, u32[]{:S(2)}) copy-start(bf16[7168,256]{1,0:T(8,128)(2,1)} %get-tuple-element.24) | copy-start | bytes 11010052
  108.4 2.0 %copy-start.6 = (bf16[7168,256]{1,0:T(8,128)(2,1)S(1)}, bf16[7168,256]{1,0:T(8,128)(2,1)}, u32[]{:S(2)}) copy-start(bf16[7168,256]{1,0:T(8,128)(2,1)} %get-tuple-element.25) | copy-start | bytes 11010052
  108.4 3.2 %copy-start.7 = (bf16[7168,256]{1,0:T(8,128)(2,1)S(1)}, bf16[7168,256]{1,0:T(8,128)(2,1)}, u32[]{:S(2)}) copy-start(bf16[7168,256]{1,0:T(8,128)(2,1)} %get-tuple-element.26) | copy-start | bytes 11010052
  111.5 2.0 %copy-start.4 = (bf16[7168,256]{1,0:T(8,128)(2,1)S(1)}, bf16[7168,256]{1,0:T(8,128)(2,1)}, u32[]{:S(2)}) copy-start(bf16[7168,256]{1,0:T(8,128)(2,1)} %get-tuple-element.27) | copy-start | bytes 11010052
  111.5 3.2 %copy-start.5 = (bf16[7168,256]{1,0:T(8,128)(2,1)S(1)}, bf16[7168,256]{1,0:T(8,128)(2,1)}, u32[]{:S(2)}) copy-start(bf16[7168,256]{1,0:T(8,128)(2,1)} %get-tuple-element.28) | copy-start | bytes 11010052
  114.7 2.0 %copy-start.2 = (bf16[7168,256]{1,0:T(8,128)(2,1)S(1)}, bf16[7168,256]{1,0:T(8,128)(2,1)}, u32[]{:S(2)}) copy-start(bf16[7168,256]{1,0:T(8,128)(2,1)} %get-tuple-element.29) | copy-start | bytes 11010052
  114.7 3.2 %copy-start.3 = (bf16[7168,256]{1,0:T(8,128)(2,1)S(1)}, bf16[7168,256]{1,0:T(8,128)(2,1)}, u32[]{:S(2)}) copy-start(bf16[7168,256]{1,0:T(8,128)(2,1)} %get-tuple-element.30) | copy-start | bytes 11010052
  117.8 2.0 %copy-start = (bf16[7168,256]{1,0:T(8,128)(2,1)S(1)}, bf16[7168,256]{1,0:T(8,128)(2,1)}, u32[]{:S(2)}) copy-start(bf16[7168,256]{1,0:T(8,128)(2,1)} %get-tuple-element.5) | copy-start | bytes 11010052
  117.8 3.2 %copy-start.1 = (bf16[7168,256]{1,0:T(8,128)(2,1)S(1)}, bf16[7168,256]{1,0:T(8,128)(2,1)}, u32[]{:S(2)}) copy-start(bf16[7168,256]{1,0:T(8,128)(2,1)} %get-tuple-element.6) | copy-start | bytes 11010052
  154.1 10.5 %copy-start.14 = (bf16[2,8]{1,0:T(2,128)(2,1)S(1)}, bf16[2,8]{1,0:T(2,128)(2,1)}, u32[]{:S(2)}) copy-start(bf16[2,8]{1,0:T(2,128)(2,1)} %param.6) | copy-start | bytes 100
  154.1 17.9 %copy-start.15 = (u32[32]{0:T(128)S(1)}, u32[32]{0:T(128)}, u32[]{:S(2)}) copy-start(u32[32]{0:T(128)} %constant.137) | copy-start | bytes 388
  159.5 19.0 %all-to-all-start.1 = ((bf16[8,4,7168]{2,1,0:T(4,128)(2,1)}), bf16[8,4,7168]{2,1,0:T(4,128)(2,1)S(1)}, u32[]{:S(2)}, u32[]{:S(2)}) async-start(bf16[8,4,7168]{2,1,0:T(4,128)(2,1)} %reshape.116), calls=%async_computation.1 | async-start | bytes 917504 | tf_op jit(solution)/shard_map/all_to_all | solution.py:103
where the time goes:
time: 203 us; the launch traced here: 199 us
  other arithmetic  69.7 us (34%)
  matrix products  50.8 us (25%)
  blocking collectives  44.5 us (22%)
  local copies, waits for them, and re-layouts  16.5 us (8%)
  starting transfers between devices  9.97 us (5%)
  waiting for transfers between devices  5.29 us (3%)
  between operations  2.45 us (1%)
    convert_element_type x1, other arithmetic, hashed_weights(): return (uniform_part * math.sqrt(12.0 / fan_in)).astype(jnp.bfloat16)  69.3 us
    dot_general x8, matrix products, apply_block(): return jnp.dot(hidden, w_down, preferred_element_type=jnp.float32)  36.2 us
    unnamed x1, blocking collectives  19.3 us
    dot_general x8, matrix products, apply_block(): jnp.dot(row_block, gate_and_up, preferred_element_type=jnp.float32)  14 us
    unnamed x34, local copies, waits for them, and re-layouts  12.2 us
    all_gather x1, blocking collectives, body(): lax.all_gather(tokens, 'local', axis=0, tiled=True)  10.1 us
    all_gather x1, blocking collectives, body(): lax.all_gather(expert_ids, 'local', axis=0, tiled=True)  7.86 us
    all_gather x1, blocking collectives, body(): lax.all_gather(gate_weights, 'local', axis=0, tiled=True)  7.17 us
  transfers between devices with their start and end apart: 2, of which 1 were waited for; matrix products, arithmetic and copies ran while one was open for 36% of the time, Pallas kernels for 0%

commit v1 on v0

--- a/solution.py
+++ b/solution.py
@@ -62,7 +62,9 @@
     hidden_block = min(quarter_width, 256)
     model_width = tokens.shape[1]
     group_rows, group_ids, group_gates = (
-        lax.all_gather(tokens, "local", axis=0, tiled=True),
+        jnp.concatenate(
+            lax.all_to_all(jnp.stack([tokens] * lax.axis_size("local")), "local", 0, 0), axis=0
+        ),
         lax.all_gather(expert_ids, "local", axis=0, tiled=True),
         lax.all_gather(gate_weights, "local", axis=0, tiled=True),
     )

time: 203 us -> 212 us (1.044)
  waiting for transfers between devices: 5.29 us -> 17.8 us
  blocking collectives: 44.5 us -> 36 us
  starting transfers between devices: 9.97 us -> 13.5 us
    all_to_all x1, waiting for transfers between devices: 0.01 us -> 13.2 us  [body(): lax.all_to_all(outgoing, 'node', split_axis=0, concat_axis=0, tiled=True)]
    all_gather x1 -> x0, blocking collectives: 10.1 us -> none  [body(): lax.all_gather(tokens, 'local', axis=0, tiled=True)]
    all_to_all x0 -> x1, starting transfers between devices: none -> 5.19 us  [body(): lax.all_to_all(jnp.stack([tokens] * lax.axis_size('local')), 'local', 0, 0)]
    unnamed x34 -> x33, local copies, waits for them, and re-layouts: 12.2 us -> 12.2 us
  transfers between devices with their start and end apart: 2 -> 3, of which waited for: 1 -> 2; matrix products, arithmetic and copies ran while one was open for 36% -> 34% of each run, Pallas kernels for 0% -> 0%
where the time goes in v1:
time: 212 us; the launch traced here: 208 us
  other arithmetic  69.6 us (33%)
  matrix products  50.8 us (24%)
  blocking collectives  36 us (17%)
  local copies, waits for them, and re-layouts  17.9 us (8%)
  waiting for transfers between devices  17.8 us (8%)
  starting transfers between devices  13.5 us (6%)
  between operations  2.46 us (1%)
    convert_element_type x1, other arithmetic, hashed_weights(): return (uniform_part * math.sqrt(12.0 / fan_in)).astype(jnp.bfloat16)  69.3 us
    dot_general x8, matrix products, apply_block(): return jnp.dot(hidden, w_down, preferred_element_type=jnp.float32)  36.2 us
    unnamed x1, blocking collectives  19.5 us
    dot_general x8, matrix products, apply_block(): jnp.dot(row_block, gate_and_up, preferred_element_type=jnp.float32)  14 us
    all_to_all x1, waiting for transfers between devices, body(): lax.all_to_all(outgoing, 'node', split_axis=0, concat_axis=0, tiled=True)  13.2 us
    unnamed x33, local copies, waits for them, and re-layouts  12.2 us
    all_gather x1, blocking collectives, body(): lax.all_gather(expert_ids, 'local', axis=0, tiled=True)  8.7 us
    all_gather x1, blocking collectives, body(): lax.all_gather(gate_weights, 'local', axis=0, tiled=True)  7.79 us
  transfers between devices with their start and end apart: 3, of which 2 were waited for; matrix products, arithmetic and copies ran while one was open for 34% of the time, Pallas kernels for 0%

profile of v1, /device:TPU:0, one launch (start us, length us, event | category | flops | bytes accessed | tf_op | source)
XLA Modules:
  0.0 208.1 jit_solution(17723465393329281470)
XLA Ops:
  0.0 1.4 stack.2
  1.4 5.2 %all-to-all-start = ((bf16[4,2,7168]{2,1,0:T(2,128)(2,1)}), bf16[4,2,7168]{2,1,0:T(2,128)(2,1)S(1)}, u32[]{:S(2)}, u32[]{:S(2)}) async-start(bf16[4,2,7168]{2,1,0:T(2,128)(2,1)} %stack.2), calls=%async_computation | async-start | bytes 229376 | tf_op jit(solution)/shard_map/all_to_all | solution.py:66
  6.7 8.7 %all-gather = s32[4,2,8]{2,1,0:T(2,128)S(1)} all-gather(s32[1,2,8]{2,1,0:T(2,128)} %bitcast.33), channel_id=1, replica_groups=mesh['node'=8,'local'=4] {'local'}, dimensions={0}, use_global_device_ids=true | all-gather | bytes 320 | tf_op jit(solution)/shard_map/all_gather | solution.py:68
  15.4 0.1 compare_reduce_fusion
  15.6 0.1 copy.16
  15.6 1.2 dynamic_slice.13
  17.5 69.3 %fusion.176 = (bf16[7168,256]{1,0:T(8,128)(2,1)}, bf16[7168,256]{1,0:T(8,128)(2,1)}, bf16[7168,256]{1,0:T(8,128)(2,1)}, bf16[7168,256]{1,0:T(8,128)(2,1)}, bf16[...) fusion(s32[256]{0:T(256)S(1)} %get-tuple-element.33, ...), kind=kLoop, calls=%fused_computation.257 | loop fusion | flops 469762048 | bytes 58756104 | tf_op jit(solution)/shard_map/convert_element_type | solution.py:22
  86.8 0.0 all-to-all-done
  86.9 0.2 convolution_convert_fusion
  87.2 1.1 copy.18
  88.3 4.9 %all-to-all-start.1 = ((bf16[8,4,7168]{2,1,0:T(4,128)(2,1)}), bf16[8,4,7168]{2,1,0:T(4,128)(2,1)S(1)}, u32[]{:S(2)}, u32[]{:S(2)}) async-start(bf16[8,4,7168]{2,1,0:T(4,128)(2,1)} %copy.18), calls=%async_computation.1 | async-start | bytes 917504 | tf_op jit(solution)/shard_map/all_to_all | solution.py:101
  93.9 13.2 %all-to-all-done.1 = bf16[8,4,7168]{2,1,0:T(4,128)(2,1)S(1)} async-done(((bf16[8,4,7168]{2,1,0:T(4,128)(2,1)}), bf16[8,4,7168]{2,1,0:T(4,128)(2,1)S(1)}, u32[]{:S(2)}, u32[]{:S(2)}) %all-to-all-start.1) | async-done | bytes 458784 | tf_op jit(solution)/shard_map/all_to_all | solution.py:101
  107.1 0.1 reshape.121
  107.2 0.0 copy-start.12
  107.2 0.0 copy-start.13
  107.2 4.5 %fusion.193 = f32[32,512]{1,0:T(8,128)S(1)} fusion(bf16[32,7168]{1,0:T(8,128)(2,1)S(1)} %reshape.121, bf16[7168,256]{1,0:T(8,128)(2,1)} %get-tuple-element.31, bf16[7168,256]{1,0:T(8,128)(2,1)} %get-tuple-element.32), kind=kOutput, calls=%fused_computation.274 | convolution fusion | flops 249561088 | bytes 7864320 | tf_op jit(solution)/shard_map/dot_general | solution.py:40
  111.8 0.0 copy-done.12
  111.8 0.7 copy-done.13
  112.5 0.0 copy-start.10
  112.5 0.0 copy-start.11
  112.5 1.3 fusion.197
  113.9 0.7 copy-done.10
  114.6 1.1 copy-done.11
  115.7 0.0 copy-start.8
  115.7 0.0 copy-start.9
  115.7 1.3 fusion.201
  117.0 0.7 copy-done.8
  117.7 1.1 copy-done.9
  118.8 0.0 copy-start.6
  118.8 0.0 copy-start.7
  118.8 1.3 fusion.205
  120.2 0.7 copy-done.6
  120.9 1.1 copy-done.7
  122.0 1.3 fusion.209
  123.3 0.7 copy-done.4
  124.0 1.1 copy-done.5
  125.2 1.3 fusion.213
  126.5 0.7 copy-done.2
  127.2 1.1 copy-done.3
  128.3 1.3 fusion.217
  129.7 0.7 copy-done
  130.4 1.1 copy-done.1
  131.5 1.3 fusion.221
  132.8 4.4 %fusion.302 = f32[32,7168]{1,0:T(8,128)S(1)} fusion(s32[256]{0:T(256)S(1)} %iota_multiply_fusion.1, s32[]{:T(128)S(6)} %add.686, f32[32,512]{1,0:T(8,128)S(1)} %fusion.193), kind=kOutput, calls=%fused_computation.384 | convolution fusion | flops 148684800 | bytes 984068 | tf_op jit(solution)/shard_map/dot_general | solution.py:44
  137.2 4.6 %convolution_add_fusion.6 = f32[32,7168]{1,0:T(8,128)S(1)} fusion(f32[32,7168]{1,0:T(8,128)S(1)} %fusion.302, s32[256]{0:T(256)S(1)} %broadcast_multiply_fusion.6, s32[]{:T(128)S(6)} %add.686, f32[32,512]{1,0:T(8,128)S(1)} %fusion.197), kind=kOutput, calls=%fused_computation.78 | convolution fusion | flops 148914176 | bytes 1901572 | tf_op jit(solution)/shard_map/dot_general | solution.py:44
  141.9 4.4 %convolution_add_fusion.5 = f32[32,7168]{1,0:T(8,128)S(1)} fusion(f32[32,7168]{1,0:T(8,128)S(1)} %convolution_add_fusion.6, s32[256]{0:T(256)S(1)} %broadcast_multiply_fusion.5, s32[]{:T(128)S(6)} %add.686, f32[32,512]{1,0:T(8,128)S(1)} %fusion.201), kind=kOutput, calls=%fused_computation.77 | convolution fusion | flops 148914176 | bytes 1901572 | tf_op jit(solution)/shard_map/dot_general | solution.py:44
  146.3 4.4 %convolution_add_fusion.4 = f32[32,7168]{1,0:T(8,128)S(1)} fusion(f32[32,7168]{1,0:T(8,128)S(1)} %convolution_add_fusion.5, s32[256]{0:T(256)S(1)} %broadcast_multiply_fusion.4, s32[]{:T(128)S(6)} %add.686, f32[32,512]{1,0:T(8,128)S(1)} %fusion.205), kind=kOutput, calls=%fused_computation.76 | convolution fusion | flops 148914176 | bytes 1901572 | tf_op jit(solution)/shard_map/dot_general | solution.py:44
  150.8 4.7 %convolution_add_fusion.3 = f32[32,7168]{1,0:T(8,128)S(1)} fusion(f32[32,7168]{1,0:T(8,128)S(1)} %convolution_add_fusion.4, s32[256]{0:T(256)S(1)} %broadcast_multiply_fusion.3, s32[]{:T(128)S(6)} %add.686, f32[32,512]{1,0:T(8,128)S(1)} %fusion.209), kind=kOutput, calls=%fused_computation.75 | convolution fusion | flops 148914176 | bytes 1901572 | tf_op jit(solution)/shard_map/dot_general | solution.py:44
  155.4 4.4 %convolution_add_fusion.2 = f32[32,7168]{1,0:T(8,128)S(1)} fusion(f32[32,7168]{1,0:T(8,128)S(1)} %convolution_add_fusion.3, s32[256]{0:T(256)S(1)} %broadcast_multiply_fusion.2, s32[]{:T(128)S(6)} %add.686, f32[32,512]{1,0:T(8,128)S(1)} %fusion.213), kind=kOutput, calls=%fused_computation.74 | convolution fusion | flops 148914176 | bytes 1901572 | tf_op jit(solution)/shard_map/dot_general | solution.py:44
  159.9 4.7 %convolution_add_fusion.1 = f32[32,7168]{1,0:T(8,128)S(1)} fusion(f32[32,7168]{1,0:T(8,128)S(1)} %convolution_add_fusion.2, s32[256]{0:T(256)S(1)} %broadcast_multiply_fusion.1, s32[]{:T(128)S(6)} %add.686, f32[32,512]{1,0:T(8,128)S(1)} %fusion.217), kind=kOutput, calls=%fused_computation.73 | convolution fusion | flops 148914176 | bytes 1901572 | tf_op jit(solution)/shard_map/dot_general | solution.py:44
  164.6 0.0 copy-start.15
  164.6 4.5 %fusion = bf16[32,7168]{1,0:T(8,128)(2,1)S(1)} fusion(f32[32,7168]{1,0:T(8,128)S(1)} %convolution_add_fusion.1, s32[256]{0:T(256)S(1)} %broadcast_multiply_fusion, s32[]{:T(128)S(6)} %add.686, f32[32,512]{1,0:T(8,128)S(1)} %fusion.221), kind=kOutput, calls=%fused_computation.79 | convolution fusion | flops 149143552 | bytes 1442820 | tf_op jit(solution)/shard_map/dot_general | solution.py:44
  169.0 0.9 reshape.122
  170.0 3.5 %all-to-all-start.2 = ((bf16[8,4,7168]{2,1,0:T(4,128)(2,1)}), bf16[8,4,7168]{2,1,0:T(4,128)(2,1)S(1)}, u32[]{:S(2)}, u32[]{:S(2)}) async-start(bf16[8,4,7168]{2,1,0:T(4,128)(2,1)} %reshape.122), calls=%async_computation.2 | async-start | bytes 917504 | tf_op jit(solution)/shard_map/all_to_all | solution.py:105
  173.5 0.0 copy-done.14
  173.5 7.8 %all-gather.1 = bf16[4,2,8]{2,1,0:T(2,128)(2,1)S(1)} all-gather(bf16[1,2,8]{2,1,0:T(2,128)(2,1)S(1)} %bitcast.34), channel_id=1, replica_groups=mesh['node'=8,'local'=4] {'local'}, dimensions={0}, use_global_device_ids=true | all-gather | bytes 160 | tf_op jit(solution)/shard_map/all_gather | solution.py:69
  181.3 0.1 fusion.307
  181.4 0.1 copy.17
  181.5 0.0 copy-done.15
  181.5 0.6 dynamic-slice
  182.7 4.6 %all-to-all-done.2 = bf16[8,4,7168]{2,1,0:T(4,128)(2,1)S(1)} async-done(((bf16[8,4,7168]{2,1,0:T(4,128)(2,1)}), bf16[8,4,7168]{2,1,0:T(4,128)(2,1)S(1)}, u32[]{:S(2)}, u32[]{:S(2)}) %all-to-all-start.2) | async-done | bytes 458784 | tf_op jit(solution)/shard_map/all_to_all | solution.py:105
  187.3 0.4 convolution_bitcast_fusion
  187.7 19.5 %all-reduce.2 = bf16[8,7168]{1,0:T(8,128)(2,1)S(1)} all-reduce(f32[8,7168]{1,0:T(8,128)S(1)} %convolution_bitcast_fusion), channel_id=2, replica_groups=mesh['node'=8,'local'=4] {'local'}, use_global_device_ids=true, to_apply=%region_3.4.clone | all-reduce | flops 57344 | bytes 344064
  207.2 0.6 dynamic-slice_convert_fusion
  (27 shorter events, 0.2 us)
Async XLA Ops:
  1.4 85.4 %all-to-all-start = ((bf16[4,2,7168]{2,1,0:T(2,128)(2,1)}), bf16[4,2,7168]{2,1,0:T(2,128)(2,1)S(1)}, u32[]{:S(2)}, u32[]{:S(2)}) async-start(bf16[4,2,7168]{2,1,0:T(2,128)(2,1)} %stack.2), calls=%async_computation | async-start | bytes 229376 | tf_op jit(solution)/shard_map/all_to_all | solution.py:66
  88.3 18.8 %all-to-all-start.1 = ((bf16[8,4,7168]{2,1,0:T(4,128)(2,1)}), bf16[8,4,7168]{2,1,0:T(4,128)(2,1)S(1)}, u32[]{:S(2)}, u32[]{:S(2)}) async-start(bf16[8,4,7168]{2,1,0:T(4,128)(2,1)} %copy.18), calls=%async_computation.1 | async-start | bytes 917504 | tf_op jit(solution)/shard_map/all_to_all | solution.py:101
  107.2 4.6 %copy-start.12 = (bf16[7168,256]{1,0:T(8,128)(2,1)S(1)}, bf16[7168,256]{1,0:T(8,128)(2,1)}, u32[]{:S(2)}) copy-start(bf16[7168,256]{1,0:T(8,128)(2,1)} %get-tuple-element.19) | copy-start | bytes 11010052
  107.2 5.3 %copy-start.13 = (bf16[7168,256]{1,0:T(8,128)(2,1)S(1)}, bf16[7168,256]{1,0:T(8,128)(2,1)}, u32[]{:S(2)}) copy-start(bf16[7168,256]{1,0:T(8,128)(2,1)} %get-tuple-element.20) | copy-start | bytes 11010052
  112.5 2.0 copy-start.10
  112.5 3.2 %copy-start.11 = (bf16[7168,256]{1,0:T(8,128)(2,1)S(1)}, bf16[7168,256]{1,0:T(8,128)(2,1)}, u32[]{:S(2)}) copy-start(bf16[7168,256]{1,0:T(8,128)(2,1)} %get-tuple-element.22) | copy-start | bytes 11010052
  115.7 2.0 copy-start.8
  115.7 3.2 %copy-start.9 = (bf16[7168,256]{1,0:T(8,128)(2,1)S(1)}, bf16[7168,256]{1,0:T(8,128)(2,1)}, u32[]{:S(2)}) copy-start(bf16[7168,256]{1,0:T(8,128)(2,1)} %get-tuple-element.24) | copy-start | bytes 11010052
  118.8 2.0 copy-start.6
  118.8 3.2 %copy-start.7 = (bf16[7168,256]{1,0:T(8,128)(2,1)S(1)}, bf16[7168,256]{1,0:T(8,128)(2,1)}, u32[]{:S(2)}) copy-start(bf16[7168,256]{1,0:T(8,128)(2,1)} %get-tuple-element.26) | copy-start | bytes 11010052
  122.0 2.0 copy-start.4
  122.0 3.2 %copy-start.5 = (bf16[7168,256]{1,0:T(8,128)(2,1)S(1)}, bf16[7168,256]{1,0:T(8,128)(2,1)}, u32[]{:S(2)}) copy-start(bf16[7168,256]{1,0:T(8,128)(2,1)} %get-tuple-element.28) | copy-start | bytes 11010052
  125.2 2.0 copy-start.2
  125.2 3.2 %copy-start.3 = (bf16[7168,256]{1,0:T(8,128)(2,1)S(1)}, bf16[7168,256]{1,0:T(8,128)(2,1)}, u32[]{:S(2)}) copy-start(bf16[7168,256]{1,0:T(8,128)(2,1)} %get-tuple-element.30) | copy-start | bytes 11010052
  128.3 2.0 copy-start
  128.3 3.2 %copy-start.1 = (bf16[7168,256]{1,0:T(8,128)(2,1)S(1)}, bf16[7168,256]{1,0:T(8,128)(2,1)}, u32[]{:S(2)}) copy-start(bf16[7168,256]{1,0:T(8,128)(2,1)} %get-tuple-element.6) | copy-start | bytes 11010052
  164.6 8.9 %copy-start.14 = (bf16[2,8]{1,0:T(2,128)(2,1)S(1)}, bf16[2,8]{1,0:T(2,128)(2,1)}, u32[]{:S(2)}) copy-start(bf16[2,8]{1,0:T(2,128)(2,1)} %param.6) | copy-start | bytes 100
  164.6 16.9 %copy-start.15 = (u32[32]{0:T(128)S(1)}, u32[32]{0:T(128)}, u32[]{:S(2)}) copy-start(u32[32]{0:T(128)} %constant.137) | copy-start | bytes 388
  170.0 17.3 %all-to-all-start.2 = ((bf16[8,4,7168]{2,1,0:T(4,128)(2,1)}), bf16[8,4,7168]{2,1,0:T(4,128)(2,1)S(1)}, u32[]{:S(2)}, u32[]{:S(2)}) async-start(bf16[8,4,7168]{2,1,0:T(4,128)(2,1)} %reshape.122), calls=%async_computation.2 | async-start | bytes 917504 | tf_op jit(solution)/shard_map/all_to_all | solution.py:105
